TPU v7x, 32 devices: a whole 2x2x4 slice. The times are simulated.
32 devices in a mesh: groups: 2 (over y), member: 4 (over x, core), fsdp: 4 (over z).
Axes of the slice: x: 2, y: 2, z: 4, core: 2. Of those that a mesh axis runs over, the one named last changes fastest.
Arguments:
- params: float32 [64, 1024, 1024], P(('groups', 'member'), 'fsdp'), parts along dimension 0, may hold values from -210 to 210
- gradients: bfloat16 [64, 1024, 1024], P(('groups', 'member'), 'fsdp'), parts along dimension 0, may hold values from -1.5258789e-05 to 1.5258789e-05
- first_moment: float32 [64, 1024, 1024], P(('groups', 'member'), 'fsdp'), parts along dimension 0, may hold values from -5.9604645e-07 to 5.9604645e-07
- second_moment: float32 [64, 1024, 1024], P(('groups', 'member'), 'fsdp'), parts along dimension 0, may hold values from 1.8189895e-15 to 3.6379787e-14
Outputs:
- new_params: float32 [64, 1024, 1024], P(('groups', 'member'), 'fsdp'), parts along dimension 0
- new_first: float32 [64, 1024, 1024], P(('groups', 'member'), 'fsdp'), parts along dimension 0
- new_second: float32 [64, 1024, 1024], P(('groups', 'member'), 'fsdp'), parts along dimension 0
- update: float32 [64, 1024, 1024], P(('groups', 'member'), 'fsdp'), parts along dimension 0
- stein_dir: float32 [64, 1024, 1024], P(('groups', 'member'), 'fsdp'), parts along dimension 0
- pair_distance: float32 [64, 32], P('groups'), parts along dimension 0
There are 2 independent parts, one for each index of `groups`. A program takes and returns all parts, laid end to end along the dimension named above; each array names one. Nothing has to cross between parts.
All inputs are finite; a program needn't handle non-finite values.
Results may differ from a plain program's by a relative error of at most 0.0025.
Values may be sent and summed in bfloat16 or wider, within the bound.
No kernel may reach another device: no remote copies, remote signals or barrier semaphores. Data moves between devices by JAX's collectives and lax.ppermute only.
A program may use at most 192 MiB of HBM per device.

v0:
```python
import math
import jax
import jax.numpy as jnp
from jax import lax
from jax.sharding import PartitionSpec as P

STEP_COUNT = 100
decay_first = 0.9
decay_second = 0.95
epsilon = 1e-08
learn_rate = 0.001
weight_decay = 0.05


def kernel_from(gram_total, members):
    self_dots = jnp.diagonal(gram_total)
    sqdist = self_dots[:, None] + self_dots[None, :] - 2.0 * gram_total
    kernel_scale = jnp.sum(sqdist) / (members * (members - 1)) / math.log(members)
    kernel = jnp.exp(-sqdist / kernel_scale)
    return (sqdist, kernel_scale, kernel.astype(jnp.bfloat16))


def adamw_step(params, stein_dir, first_moment, second_moment):
    descent = -stein_dir
    new_first = decay_first * first_moment + (1.0 - decay_first) * descent
    new_second = decay_second * second_moment + (1.0 - decay_second) * descent * descent
    first_hat = new_first / (1.0 - decay_first**STEP_COUNT)
    second_hat = new_second / (1.0 - decay_second**STEP_COUNT)
    update = first_hat / (jnp.sqrt(second_hat) + epsilon) + weight_decay * params
    new_params = params - learn_rate * update
    return (new_params, new_first, new_second, update)


def inner_products(left_flat, right_flat):
    return lax.dot_general(
        left_flat, right_flat, (((1,), (1,)), ((), ())), preferred_element_type=jnp.float32
    )


def shards(params, gradients, first_moment, second_moment):
    members_dev, rows_dev, feature_width = params.shape
    n_member = lax.axis_size("member")
    members = members_dev * n_member
    entries = rows_dev * lax.axis_size("fsdp") * feature_width
    working = params.astype(jnp.bfloat16)
    ascent = -gradients
    wide_work, wide_ascent = (
        lax.all_to_all(working, "member", split_axis=1, concat_axis=0, tiled=True),
        lax.all_to_all(ascent, "member", split_axis=1, concat_axis=0, tiled=True),
    )
    flat_work = wide_work.reshape(members, -1)
    gram_local = inner_products(flat_work, flat_work)
    flat_ascent = wide_ascent.reshape(members, -1)
    gram_total = lax.psum(gram_local, ("member", "fsdp"))
    sqdist, kernel_scale, kernel_half = kernel_from(gram_total, members)
    rowsum = jnp.sum(kernel_half.astype(jnp.float32), axis=1)
    repulse = 2.0 / kernel_scale
    mixed_ascent = jnp.dot(kernel_half, flat_ascent, preferred_element_type=jnp.float32)
    mixed_work = jnp.dot(kernel_half, flat_work, preferred_element_type=jnp.float32)
    stein_mix = (
        mixed_ascent + repulse * (rowsum[:, None] * flat_work.astype(jnp.float32) - mixed_work)
    ) / members
    stein_dir = lax.all_to_all(
        stein_mix.reshape(wide_work.shape), "member", split_axis=0, concat_axis=1, tiled=True
    )
    new_params, new_first, new_second, update = adamw_step(
        params, stein_dir, first_moment, second_moment
    )
    pair_distance = sqdist / entries
    return (new_params, new_first, new_second, update, stein_dir, pair_distance)


def solution(mesh):
    return jax.shard_map(
        shards,
        mesh=mesh,
        in_specs=(
            P(("groups", "member"), "fsdp", None),
            P(("groups", "member"), "fsdp", None),
            P(("groups", "member"), "fsdp", None),
            P(("groups", "member"), "fsdp", None),
        ),
        out_specs=(
            P(("groups", "member"), "fsdp", None),
            P(("groups", "member"), "fsdp", None),
            P(("groups", "member"), "fsdp", None),
            P(("groups", "member"), "fsdp", None),
            P(("groups", "member"), "fsdp", None),
            P("groups", None),
        ),
        check_vma=False,
    )
```

profile of v0, /device:TPU:0, one launch (start us, length us, event | category | flops | bytes accessed | tf_op | source)
XLA Modules:
  0.0 314.9 jit_solution(15781765817421736851)
XLA Ops:
  0.6 6.6 %copy_negate_fusion = bf16[8,256,1024]{2,0,1:T(8,128)(2,1)} fusion(bf16[8,256,1024]{2,1,0:T(8,128)(2,1)} %param.5), kind=kLoop, calls=%fused_computation.12 | loop fusion | flops 2097152 | bytes 8388608 | tf_op jit(solution)/shard_map/neg | solution.py:46
  7.3 4.8 %all-to-all-start.1 = ((bf16[8,256,1024]{2,0,1:T(8,128)(2,1)}), bf16[8,256,1024]{2,0,1:T(8,128)(2,1)}, u32[]{:S(2)}, u32[]{:S(2)}) async-start(bf16[8,256,1024]{2,0,1:T(8,128)(2,1)} %copy_negate_fusion), calls=%async_computation.1 | async-start | bytes 8388608 | tf_op jit(solution)/shard_map/all_to_all | solution.py:49
  12.1 9.8 %copy.24 = bf16[8,256,1024]{2,0,1:T(8,128)(2,1)} copy(f32[8,256,1024]{2,1,0:T(8,128)} %param.4) | data formatting | bytes 12582912 | tf_op args[0]
  22.0 39.0 %all-to-all-done.1 = bf16[8,256,1024]{2,0,1:T(8,128)(2,1)} async-done(((bf16[8,256,1024]{2,0,1:T(8,128)(2,1)}), bf16[8,256,1024]{2,0,1:T(8,128)(2,1)}, u32[]{:S(2)}, u32[]{:S(2)}) %all-to-all-start.1) | async-done | bytes 4194336 | tf_op jit(solution)/shard_map/all_to_all | solution.py:49
  61.0 5.0 %all-to-all-start = ((bf16[8,256,1024]{2,0,1:T(8,128)(2,1)}), bf16[8,256,1024]{2,0,1:T(8,128)(2,1)}, u32[]{:S(2)}, u32[]{:S(2)}) async-start(bf16[8,256,1024]{2,0,1:T(8,128)(2,1)} %copy.24), calls=%async_computation | async-start | bytes 8388608 | tf_op jit(solution)/shard_map/all_to_all | solution.py:48
  66.0 4.5 %copy.25 = bf16[8,4,64,1024]{3,2,0,1:T(8,128)(2,1)S(1)} copy(bf16[8,4,64,1024]{3,0,2,1:T(8,128)(2,1)} %bitcast.4) | data formatting | bytes 8388608 | tf_op jit(solution)/shard_map/all_to_all | solution.py:49
  70.5 4.3 %copy.19 = bf16[4,8,64,1024]{3,1,2,0:T(8,128)(2,1)} copy(bf16[4,8,64,1024]{3,2,1,0:T(8,128)(2,1)S(1)} %bitcast.34) | data formatting | bytes 8388608
  74.9 39.2 %all-to-all-done = bf16[8,256,1024]{2,0,1:T(8,128)(2,1)} async-done(((bf16[8,256,1024]{2,0,1:T(8,128)(2,1)}), bf16[8,256,1024]{2,0,1:T(8,128)(2,1)}, u32[]{:S(2)}, u32[]{:S(2)}) %all-to-all-start) | async-done | bytes 4194336 | tf_op jit(solution)/shard_map/all_to_all | solution.py:48
  114.1 4.7 %fusion.6 = f32[32,32]{1,0:T(8,128)S(1)} fusion(bf16[32,65536]{1,0:T(8,128)(2,1)} %bitcast.2), kind=kOutput, calls=%fused_computation.19 | convolution fusion | flops 134217728 | bytes 4198400 | tf_op jit(solution)/shard_map/dot_general | solution.py:35
  118.7 61.5 %psum.7 = f32[32,32]{1,0:T(8,128)S(1)} all-reduce(f32[32,32]{1,0:T(8,128)S(1)} %fusion.6), channel_id=1, replica_groups=mesh['groups'=2,'member'=4,'fsdp'=4] {'member','fsdp'}, use_global_device_ids=true, to_apply=%region_0.0 | all-reduce | flops 1024 | bytes 8192 | tf_op jit(solution)/shard_map/psum | solution.py:54
  180.2 0.7 gather_fusion
  180.9 1.3 fusion.3
  182.8 0.2 convert_reduce_fusion
  183.1 0.0 copy-start
  183.1 5.1 %fusion = f32[32,65536]{1,0:T(8,128)S(1)} fusion(bf16[32,32]{1,0:T(8,128)(2,1)S(1)} %get-tuple-element.11, bf16[32,65536]{1,0:T(8,128)(2,1)} %bitcast.2, f32[32]{0:T(128)S(1)} %get-tuple-element.10, f32[]{:T(128)S(6)} %div.43), kind=kOutput, calls=%fused_computation.2 | convolution fusion | flops 142606336 | bytes 12585092 | tf_op jit(solution)/shard_map/dot_general | solution.py:59
  188.2 0.0 copy-done
  188.2 1.2 fusion.1
  189.4 4.9 %copy.20 = f32[4,8,64,1024]{3,2,1,0:T(8,128)S(1)} copy(f32[4,8,64,1024]{3,1,2,0:T(8,128)S(1)} %bitcast.27) | data formatting | bytes 16777216
  194.3 0.0 slice-start
  194.3 96.1 %all_to_all.48 = f32[32,64,1024]{2,1,0:T(8,128)S(1)} all-to-all(f32[32,64,1024]{2,1,0:T(8,128)S(1)} %bitcast.28), channel_id=1, replica_groups=mesh['groups'=2,'member'=4,'fsdp'=4] {'member'}, dimensions={0} | all-to-all | bytes 16777216 | tf_op jit(solution)/shard_map/all_to_all | solution.py:63
  290.4 0.0 slice-start.1
  290.4 4.3 %copy.18 = f32[4,8,64,1024]{3,2,0,1:T(8,128)} copy(f32[4,8,64,1024]{3,2,1,0:T(8,128)S(1)} %bitcast.29) | data formatting | bytes 16777216 | tf_op jit(solution)/shard_map/all_to_all | solution.py:63
  294.7 0.0 slice-done
  294.7 0.0 slice-done.1
  294.7 20.2 %multiply_subtract_fusion = (f32[8,256,1024]{2,1,0:T(8,128)}, f32[8,256,1024]{2,1,0:T(8,128)}, f32[8,256,1024]{2,1,0:T(8,128)}, f32[8,256,1024]{2,1,0:T(8,128)}) fusion(f32[8,256,1024]{2,1,0:T(8,128)S(1)} %bitcast.31, f32[8,256,1024]{2,1,0:T(8,128)} %param.6, f32[8,256,1024]{2,1,0:T(8,128)} %param.7, f32[4,8,64,1024]{3,2,0,1:T(8,128)} %copy.18), kind=kLoop, calls=%fused_computation.8 | loop fusion | flops 33554432 | bytes 67108864 | tf_op jit(solution)/shard_map/sub | solution.py:30
  (2 shorter events, 0.0 us)
Async XLA Ops:
  7.3 53.7 %all-to-all-start.1 = ((bf16[8,256,1024]{2,0,1:T(8,128)(2,1)}), bf16[8,256,1024]{2,0,1:T(8,128)(2,1)}, u32[]{:S(2)}, u32[]{:S(2)}) async-start(bf16[8,256,1024]{2,0,1:T(8,128)(2,1)} %copy_negate_fusion), calls=%async_computation.1 | async-start | bytes 8388608 | tf_op jit(solution)/shard_map/all_to_all | solution.py:49
  61.0 53.1 %all-to-all-start = ((bf16[8,256,1024]{2,0,1:T(8,128)(2,1)}), bf16[8,256,1024]{2,0,1:T(8,128)(2,1)}, u32[]{:S(2)}, u32[]{:S(2)}) async-start(bf16[8,256,1024]{2,0,1:T(8,128)(2,1)} %copy.24), calls=%async_computation | async-start | bytes 8388608 | tf_op jit(solution)/shard_map/all_to_all | solution.py:48
  183.1 5.1 %copy-start = (bf16[4,8,64,1024]{3,1,2,0:T(8,128)(2,1)S(1)}, bf16[4,8,64,1024]{3,1,2,0:T(8,128)(2,1)}, u32[]{:S(2)}) copy-start(bf16[4,8,64,1024]{3,1,2,0:T(8,128)(2,1)} %copy.19) | copy-start | bytes 12582916
  194.3 100.4 %slice-start = ((s8[8388608]{0:T(1024)(128)(4,1)}), s8[4194304]{0:T(1024)(128)(4,1)S(1)}, s32[]{:S(2)}) async-start(s8[8388608]{0:T(1024)(128)(4,1)} %bitcast.30), calls=%async_computation.3 | async-start | bytes 8388608
  290.4 4.3 %slice-start.1 = ((s8[8388608]{0:T(1024)(128)(4,1)}), s8[4194304]{0:T(1024)(128)(4,1)S(1)}, s32[]{:S(2)}) async-start(s8[8388608]{0:T(1024)(128)(4,1)} %bitcast.30), calls=%async_computation.4 | async-start | bytes 8388608
where the time goes:
time: 315 us
  blocking collectives  158 us (50%)
  waiting for transfers between devices  78.2 us (25%)
  local copies, waits for them, and re-layouts  28.6 us (9%)
  other arithmetic  28.3 us (9%)
  matrix products  11 us (3%)
  starting transfers between devices  9.86 us (3%)
    all_to_all x1, blocking collectives, shards(): lax.all_to_all(stein_mix.reshape(wide_work.shape), 'member', split_axis=0...  96.1 us
    psum x1, blocking collectives, shards(): gram_total = lax.psum(gram_local, ('member', 'fsdp'))  61.5 us
    all_to_all x1, waiting for transfers between devices, shards(): lax.all_to_all(working, 'member', split_axis=1, concat_axis=0, tiled=True)  39.2 us
    all_to_all x1, waiting for transfers between devices, shards(): lax.all_to_all(ascent, 'member', split_axis=1, concat_axis=0, tiled=True)  39 us
    sub x1, other arithmetic, adamw_step(): new_params = params - learn_rate * update  20.2 us
    unnamed x9, local copies, waits for them, and re-layouts  19.1 us
    neg x1, other arithmetic, shards(): ascent = -gradients  6.63 us
  transfers between devices with their start and end apart: 2, of which 2 were waited for; matrix products, arithmetic and copies ran while one was open for 6% of the time, Pallas kernels for 0%

commit v1 on v0

--- a/solution.py
+++ b/solution.py
@@ -51,7 +51,7 @@
     flat_work = wide_work.reshape(members, -1)
     gram_local = inner_products(flat_work, flat_work)
     flat_ascent = wide_ascent.reshape(members, -1)
-    gram_total = lax.psum(gram_local, ("member", "fsdp"))
+    gram_total = jnp.sum(lax.all_gather(gram_local, ("member", "fsdp")), axis=0)
     sqdist, kernel_scale, kernel_half = kernel_from(gram_total, members)
     rowsum = jnp.sum(kernel_half.astype(jnp.float32), axis=1)
     repulse = 2.0 / kernel_scale

time: 315 us -> 289 us (0.917)
  blocking collectives: 158 us -> 131 us
    psum x1 -> x0, blocking collectives: 61.5 us -> none  [shards(): gram_total = lax.psum(gram_local, ('member', 'fsdp'))]
    all_gather x0 -> x1, blocking collectives: none -> 34.7 us  [shards(): gram_total = jnp.sum(lax.all_gather(gram_local, ('member', 'fsdp')), axis=0)]
where the time goes in v1:
time: 289 us; the launch traced here: 288 us
  blocking collectives  131 us (45%)
  waiting for transfers between devices  78.2 us (27%)
  local copies, waits for them, and re-layouts  28.6 us (10%)
  other arithmetic  28.3 us (10%)
  matrix products  11 us (4%)
  starting transfers between devices  9.86 us (3%)
    all_to_all x1, blocking collectives, shards(): lax.all_to_all(stein_mix.reshape(wide_work.shape), 'member', split_axis=0...  96.1 us
    all_to_all x1, waiting for transfers between devices, shards(): lax.all_to_all(working, 'member', split_axis=1, concat_axis=0, tiled=True)  39.2 us
    all_to_all x1, waiting for transfers between devices, shards(): lax.all_to_all(ascent, 'member', split_axis=1, concat_axis=0, tiled=True)  39 us
    all_gather x1, blocking collectives, shards(): gram_total = jnp.sum(lax.all_gather(gram_local, ('member', 'fsdp')), axis=0)  34.7 us
    sub x1, other arithmetic, adamw_step(): new_params = params - learn_rate * update  20.2 us
    unnamed x9, local copies, waits for them, and re-layouts  19.1 us
    neg x1, other arithmetic, shards(): ascent = -gradients  6.63 us
  transfers between devices with their start and end apart: 2, of which 2 were waited for; matrix products, arithmetic and copies ran while one was open for 6% of the time, Pallas kernels for 0%

profile of v1, /device:TPU:0, one launch (start us, length us, event | category | flops | bytes accessed | tf_op | source)
XLA Modules:
  0.0 288.2 jit_solution(12498315034920997891)
XLA Ops:
  0.6 6.6 %copy_negate_fusion = bf16[8,256,1024]{2,0,1:T(8,128)(2,1)} fusion(bf16[8,256,1024]{2,1,0:T(8,128)(2,1)} %param.5), kind=kLoop, calls=%fused_computation.12 | loop fusion | flops 2097152 | bytes 8388608 | tf_op jit(solution)/shard_map/neg | solution.py:46
  7.3 4.8 %all-to-all-start.1 = ((bf16[8,256,1024]{2,0,1:T(8,128)(2,1)}), bf16[8,256,1024]{2,0,1:T(8,128)(2,1)}, u32[]{:S(2)}, u32[]{:S(2)}) async-start(bf16[8,256,1024]{2,0,1:T(8,128)(2,1)} %copy_negate_fusion), calls=%async_computation.1 | async-start | bytes 8388608 | tf_op jit(solution)/shard_map/all_to_all | solution.py:49
  12.1 9.8 %copy.24 = bf16[8,256,1024]{2,0,1:T(8,128)(2,1)} copy(f32[8,256,1024]{2,1,0:T(8,128)} %param.4) | data formatting | bytes 12582912 | tf_op args[0]
  22.0 39.0 %all-to-all-done.1 = bf16[8,256,1024]{2,0,1:T(8,128)(2,1)} async-done(((bf16[8,256,1024]{2,0,1:T(8,128)(2,1)}), bf16[8,256,1024]{2,0,1:T(8,128)(2,1)}, u32[]{:S(2)}, u32[]{:S(2)}) %all-to-all-start.1) | async-done | bytes 4194336 | tf_op jit(solution)/shard_map/all_to_all | solution.py:49
  61.0 5.0 %all-to-all-start = ((bf16[8,256,1024]{2,0,1:T(8,128)(2,1)}), bf16[8,256,1024]{2,0,1:T(8,128)(2,1)}, u32[]{:S(2)}, u32[]{:S(2)}) async-start(bf16[8,256,1024]{2,0,1:T(8,128)(2,1)} %copy.24), calls=%async_computation | async-start | bytes 8388608 | tf_op jit(solution)/shard_map/all_to_all | solution.py:48
  66.0 4.5 %copy.25 = bf16[8,4,64,1024]{3,2,0,1:T(8,128)(2,1)S(1)} copy(bf16[8,4,64,1024]{3,0,2,1:T(8,128)(2,1)} %bitcast.5) | data formatting | bytes 8388608 | tf_op jit(solution)/shard_map/all_to_all | solution.py:49
  70.5 4.3 %copy.19 = bf16[4,8,64,1024]{3,1,2,0:T(8,128)(2,1)} copy(bf16[4,8,64,1024]{3,2,1,0:T(8,128)(2,1)S(1)} %bitcast.35) | data formatting | bytes 8388608
  74.9 39.2 %all-to-all-done = bf16[8,256,1024]{2,0,1:T(8,128)(2,1)} async-done(((bf16[8,256,1024]{2,0,1:T(8,128)(2,1)}), bf16[8,256,1024]{2,0,1:T(8,128)(2,1)}, u32[]{:S(2)}, u32[]{:S(2)}) %all-to-all-start) | async-done | bytes 4194336 | tf_op jit(solution)/shard_map/all_to_all | solution.py:48
  114.1 4.7 %fusion.6 = f32[32,32]{1,0:T(8,128)S(1)} fusion(bf16[32,65536]{1,0:T(8,128)(2,1)} %bitcast.2), kind=kOutput, calls=%fused_computation.19 | convolution fusion | flops 134217728 | bytes 4198400 | tf_op jit(solution)/shard_map/dot_general | solution.py:35
  118.7 34.7 %all-gather = f32[512,32]{1,0:T(8,128)S(1)} all-gather(f32[32,32]{1,0:T(8,128)S(1)} %fusion.6), channel_id=2, replica_groups=mesh['groups'=2,'member'=4,'fsdp'=4] {'member','fsdp'}, dimensions={0}, use_global_device_ids=true | all-gather | bytes 69632 | tf_op jit(solution)/shard_map/all_gather | solution.py:54
  153.4 0.7 gather_fusion
  154.2 1.3 fusion.3
  156.1 0.2 convert_reduce_fusion
  156.3 0.0 copy-start
  156.3 5.1 %fusion = f32[32,65536]{1,0:T(8,128)S(1)} fusion(bf16[32,32]{1,0:T(8,128)(2,1)S(1)} %get-tuple-element.11, bf16[32,65536]{1,0:T(8,128)(2,1)} %bitcast.2, f32[32]{0:T(128)S(1)} %get-tuple-element.10, f32[]{:T(128)S(6)} %div.43), kind=kOutput, calls=%fused_computation.2 | convolution fusion | flops 142606336 | bytes 12585092 | tf_op jit(solution)/shard_map/dot_general | solution.py:59
  161.4 0.0 copy-done
  161.4 1.2 fusion.1
  162.7 4.9 %copy.20 = f32[4,8,64,1024]{3,2,1,0:T(8,128)S(1)} copy(f32[4,8,64,1024]{3,1,2,0:T(8,128)S(1)} %bitcast.28) | data formatting | bytes 16777216
  167.5 0.0 slice-start
  167.6 96.1 %all_to_all.48 = f32[32,64,1024]{2,1,0:T(8,128)S(1)} all-to-all(f32[32,64,1024]{2,1,0:T(8,128)S(1)} %bitcast.29), channel_id=1, replica_groups=mesh['groups'=2,'member'=4,'fsdp'=4] {'member'}, dimensions={0} | all-to-all | bytes 16777216 | tf_op jit(solution)/shard_map/all_to_all | solution.py:63
  263.7 0.0 slice-start.1
  263.7 4.3 %copy.18 = f32[4,8,64,1024]{3,2,0,1:T(8,128)} copy(f32[4,8,64,1024]{3,2,1,0:T(8,128)S(1)} %bitcast.30) | data formatting | bytes 16777216 | tf_op jit(solution)/shard_map/all_to_all | solution.py:63
  267.9 0.0 slice-done
  268.0 0.0 slice-done.1
  268.0 20.2 %multiply_subtract_fusion = (f32[8,256,1024]{2,1,0:T(8,128)}, f32[8,256,1024]{2,1,0:T(8,128)}, f32[8,256,1024]{2,1,0:T(8,128)}, f32[8,256,1024]{2,1,0:T(8,128)}) fusion(f32[8,256,1024]{2,1,0:T(8,128)S(1)} %bitcast.32, f32[8,256,1024]{2,1,0:T(8,128)} %param.6, f32[8,256,1024]{2,1,0:T(8,128)} %param.7, f32[4,8,64,1024]{3,2,0,1:T(8,128)} %copy.18), kind=kLoop, calls=%fused_computation.8 | loop fusion | flops 33554432 | bytes 67108864 | tf_op jit(solution)/shard_map/sub | solution.py:30
  (3 shorter events, 0.0 us)
Async XLA Ops:
  7.3 53.7 %all-to-all-start.1 = ((bf16[8,256,1024]{2,0,1:T(8,128)(2,1)}), bf16[8,256,1024]{2,0,1:T(8,128)(2,1)}, u32[]{:S(2)}, u32[]{:S(2)}) async-start(bf16[8,256,1024]{2,0,1:T(8,128)(2,1)} %copy_negate_fusion), calls=%async_computation.1 | async-start | bytes 8388608 | tf_op jit(solution)/shard_map/all_to_all | solution.py:49
  61.0 53.1 %all-to-all-start = ((bf16[8,256,1024]{2,0,1:T(8,128)(2,1)}), bf16[8,256,1024]{2,0,1:T(8,128)(2,1)}, u32[]{:S(2)}, u32[]{:S(2)}) async-start(bf16[8,256,1024]{2,0,1:T(8,128)(2,1)} %copy.24), calls=%async_computation | async-start | bytes 8388608 | tf_op jit(solution)/shard_map/all_to_all | solution.py:48
  156.3 5.1 %copy-start = (bf16[4,8,64,1024]{3,1,2,0:T(8,128)(2,1)S(1)}, bf16[4,8,64,1024]{3,1,2,0:T(8,128)(2,1)}, u32[]{:S(2)}) copy-start(bf16[4,8,64,1024]{3,1,2,0:T(8,128)(2,1)} %copy.19) | copy-start | bytes 12582916
  167.5 100.4 %slice-start = ((s8[8388608]{0:T(1024)(128)(4,1)}), s8[4194304]{0:T(1024)(128)(4,1)S(1)}, s32[]{:S(2)}) async-start(s8[8388608]{0:T(1024)(128)(4,1)} %bitcast.31), calls=%async_computation.3 | async-start | bytes 8388608
  263.7 4.3 %slice-start.1 = ((s8[8388608]{0:T(1024)(128)(4,1)}), s8[4194304]{0:T(1024)(128)(4,1)S(1)}, s32[]{:S(2)}) async-start(s8[8388608]{0:T(1024)(128)(4,1)} %bitcast.31), calls=%async_computation.4 | async-start | bytes 8388608
